TPU v7x, 512 devices: a whole 4x8x8 slice. The times are simulated.
512 devices in a mesh: row: 128 (over z, y_lo, x), ch: 4 (over y_hi, core).
Axes of the slice: x: 4, y: 8 (y_hi: 2, y_lo: 4; y = y_hi * 4 + y_lo), z: 8, core: 2. Of those that a mesh axis runs over, the one named last changes fastest.
Arguments:
- tokens: bfloat16 [384, 128, 512], P('row', None, 'ch'), may hold values from -6 to 6
- conv_weight: float32 [7, 7, 512], P(None, None, 'ch'), may hold values from -0.875 to 0.875
- spectral_filter: bfloat16 [2, 384, 128, 512], P(None, None, 'row', 'ch'), may hold values from -5 to 5
- cotangent: bfloat16 [384, 128, 512], P('row', None, 'ch'), may hold values from -6 to 6
Outputs:
- filtered: bfloat16 [384, 128, 512], P('row', None, 'ch')
- token_grad: bfloat16 [384, 128, 512], P('row', None, 'ch')
- filter_grad: float32 [2, 384, 128, 512], P(None, None, 'row', 'ch')
- conv_grad: float32 [7, 7, 512], P(None, None, 'ch')
All inputs are finite; a program needn't handle non-finite values.
Results may differ from a plain program's by a relative error of at most 0.005.
Values may be sent and summed in bfloat16 or wider, within the bound.
A program may use at most 64 MiB of HBM per device.

v0:
```python
import math

import jax
import jax.numpy as jnp
from jax import lax
from jax.sharding import PartitionSpec as P

HIGHEST = lax.Precision.HIGHEST


def extended(block, sides, width):
    for axis, dim in sides:
        count = lax.axis_size(axis)
        forward = [(i, i + 1) for i in range(count - 1)]
        backward = [(target, source) for source, target in forward]
        low = lax.ppermute(
            lax.slice_in_dim(block, block.shape[dim] - width, None, axis=dim), axis, forward
        )
        high = lax.ppermute(lax.slice_in_dim(block, 0, width, axis=dim), axis, backward)
        block = jnp.concatenate([low, block, high], axis=dim)
    return block


def tables(length):
    index = jnp.arange(length, dtype=jnp.int32)
    product = index[:, None] * index[None, :] % length
    angle = product.astype(jnp.float32) * (2.0 * math.pi / length)
    return (jnp.cos(angle), jnp.sin(angle))


def depthwise(padded, weight, row_count, col_count):
    total = jnp.zeros((row_count, col_count, weight.shape[2]), jnp.float32)
    for shift_row in range(7):
        for shift_col in range(7):
            total = (
                total
                + weight[shift_row, shift_col]
                * padded[shift_row : shift_row + row_count, shift_col : shift_col + col_count]
            )
    return total


def along_cols(field, table):
    return jnp.einsum("rwc,wk->rkc", field, table, precision=HIGHEST)


def along_rows(table, field):
    return jnp.einsum("kh,hlc->klc", table, field, precision=HIGHEST)


def to_spectrum(real_part, imag_part, cosine_rows, sine_rows):
    out_re = along_rows(cosine_rows, real_part) + along_rows(sine_rows, imag_part)
    out_im = along_rows(cosine_rows, imag_part) - along_rows(sine_rows, real_part)
    return (out_re, out_im)


def from_spectrum(real_part, imag_part, cosine_rows, sine_rows):
    out_re = along_rows(cosine_rows, real_part) - along_rows(sine_rows, imag_part)
    out_im = along_rows(cosine_rows, imag_part) + along_rows(sine_rows, real_part)
    return (out_re, out_im)


def weight_terms(field_grad, padded, row_count, col_count):
    return jnp.stack(
        [
            jnp.stack(
                [
                    jnp.sum(field_grad * padded[a : a + row_count, b : b + col_count], axis=(0, 1))
                    for b in range(7)
                ]
            )
            for a in range(7)
        ]
    )


def row_tiles(tokens, conv_weight, spectral_filter, cotangent):
    row_count, col_count, chan_count = tokens.shape
    height = row_count * lax.axis_size("row")
    inverse_count = 1.0 / (height * col_count)
    cosine_cols, sine_cols = tables(col_count)
    cosine_rows, sine_rows = tables(height)
    token_rim = extended(tokens, (("row", 0),), 3)
    padded = jnp.pad(token_rim.astype(jnp.float32), ((0, 0), (3, 3), (0, 0)))
    conv_out = depthwise(padded, conv_weight, row_count, col_count)
    field_re = along_cols(conv_out, cosine_cols)
    field_im = -along_cols(conv_out, sine_cols)
    cot_float = cotangent.astype(jnp.float32)
    cot_re = along_cols(cot_float, cosine_cols)
    cot_im = -along_cols(cot_float, sine_cols)
    filt_re = spectral_filter[0].astype(jnp.float32)
    filt_im = spectral_filter[1].astype(jnp.float32)
    slab_re, slab_im = (
        lax.all_to_all(field_re, "row", split_axis=1, concat_axis=0, tiled=True),
        lax.all_to_all(field_im, "row", split_axis=1, concat_axis=0, tiled=True),
    )
    spec_re, spec_im = to_spectrum(slab_re, slab_im, cosine_rows, sine_rows)
    prod_re = filt_re * spec_re - filt_im * spec_im
    prod_im = filt_re * spec_im + filt_im * spec_re
    inv_re, inv_im = from_spectrum(prod_re, prod_im, cosine_rows, sine_rows)
    tile_re, tile_im = (
        lax.all_to_all(inv_re, "row", split_axis=0, concat_axis=1, tiled=True),
        lax.all_to_all(inv_im, "row", split_axis=0, concat_axis=1, tiled=True),
    )
    cslab_re, cslab_im = (
        lax.all_to_all(cot_re, "row", split_axis=1, concat_axis=0, tiled=True),
        lax.all_to_all(cot_im, "row", split_axis=1, concat_axis=0, tiled=True),
    )
    grad_re, grad_im = to_spectrum(cslab_re, cslab_im, cosine_rows, sine_rows)
    grad_re = grad_re * inverse_count
    grad_im = grad_im * inverse_count
    back_re = grad_re * filt_re + grad_im * filt_im
    back_im = grad_im * filt_re - grad_re * filt_im
    ginv_re, ginv_im = from_spectrum(back_re, back_im, cosine_rows, sine_rows)
    gtile_re, gtile_im = (
        lax.all_to_all(ginv_re, "row", split_axis=0, concat_axis=1, tiled=True),
        lax.all_to_all(ginv_im, "row", split_axis=0, concat_axis=1, tiled=True),
    )
    filter_grad = jnp.stack(
        [grad_re * spec_re + grad_im * spec_im, grad_im * spec_re - grad_re * spec_im]
    )
    filtered = (
        (along_cols(tile_re, cosine_cols) - along_cols(tile_im, sine_cols)) * inverse_count
    ).astype(jnp.bfloat16)
    field_grad = along_cols(gtile_re, cosine_cols) - along_cols(gtile_im, sine_cols)
    grad_rim = extended(field_grad, (("row", 0),), 3)
    grad_pad = jnp.pad(grad_rim, ((0, 0), (3, 3), (0, 0)))
    token_grad = depthwise(grad_pad, conv_weight[::-1, ::-1], row_count, col_count).astype(
        jnp.bfloat16
    )
    partial_grad = weight_terms(field_grad, padded, row_count, col_count)
    conv_grad = lax.psum(partial_grad, "row") / math.sqrt(height * col_count)
    return (filtered, token_grad, filter_grad, conv_grad)


def per_device(tokens, conv_weight, spectral_filter, cotangent):
    return row_tiles(tokens, conv_weight, spectral_filter, cotangent)


def solution(mesh):
    in_specs = (
        P("row", None, "ch"),
        P(None, None, "ch"),
        P(None, None, "row", "ch"),
        P("row", None, "ch"),
    )
    out_specs = (
        P("row", None, "ch"),
        P("row", None, "ch"),
        P(None, None, "row", "ch"),
        P(None, None, "ch"),
    )
    return jax.shard_map(
        per_device, mesh=mesh, in_specs=in_specs, out_specs=out_specs, check_vma=False
    )
```

profile of v0, /device:TPU:56, one launch (start us, length us, event | category | flops | bytes accessed | tf_op | source)
XLA Modules:
  0.0 941.9 jit_solution(396163082504076539)
XLA Ops:
  0.6 3.5 collective-permute-start
  4.2 4.6 collective-permute-start.1
  9.2 0.8 copy.29
  10.1 18.6 %all-to-all-start.5 = ((f32[3,128,128]{2,0,1:T(4,128)}), f32[3,128,128]{2,0,1:T(4,128)S(1)}, u32[]{:S(2)}, u32[]{:S(2)}) async-start(f32[3,128,128]{2,0,1:T(4,128)} %copy.29), calls=%async_computation.5 | async-start | bytes 524288 | tf_op jit(solution)/shard_map/all_to_all | solution.py:107
  29.2 0.8 copy.28
  30.2 1.0 multiply_add_fusion
  31.1 0.6 convolution_bitcast_fusion.1
  31.7 0.8 copy.22
  32.6 8.1 all-to-all-done.5
  40.6 8.2 all-to-all-start.4
  48.8 0.6 fusion.5
  49.4 0.8 copy.23
  50.3 3.6 fusion.19
  53.9 6.9 all-to-all-done.4
  60.8 9.0 all-to-all-start
  69.9 3.6 fusion.21
  73.5 3.6 fusion.3
  77.1 3.6 fusion.2
  80.7 2.9 fusion.15
  83.7 3.6 convolution_add_fusion
  87.3 14.4 %all-to-all-start.1 = ((f32[3,128,128]{2,0,1:T(4,128)}), f32[3,128,128]{2,0,1:T(4,128)S(1)}, u32[]{:S(2)}, u32[]{:S(2)}) async-start(f32[3,128,128]{2,0,1:T(4,128)} %copy.23), calls=%async_computation.1 | async-start | bytes 524288 | tf_op jit(solution)/shard_map/all_to_all | solution.py:95
  101.7 2.9 fusion.17
  104.7 3.6 convolution_subtract_fusion.1
  108.4 4.8 all-to-all-done.1
  113.2 9.3 all-to-all-start.6
  122.6 3.6 fusion.27
  126.2 3.6 fusion.29
  129.8 3.6 convolution_subtract_fusion.5
  133.4 3.8 convolution_add_fusion.3
  137.2 2.9 fusion.23
  140.2 3.6 convolution_add_fusion.2
  143.8 2.9 fusion.25
  146.8 14.4 %all-to-all-start.7 = ((f32[384,1,128]{2,1,0:T(1,128)}), f32[384,1,128]{2,1,0:T(1,128)S(1)}, u32[]{:S(2)}, u32[]{:S(2)}) async-start(f32[384,1,128]{2,1,0:T(1,128)} %bitcast.84), calls=%async_computation.7 | async-start | bytes 393216 | tf_op jit(solution)/shard_map/all_to_all | solution.py:117
  161.3 3.6 convolution_subtract_fusion.4
  164.9 0.8 pad_maximum_fusion
  165.7 0.6 fusion.147
  166.3 5.5 all-to-all-done.7
  171.7 8.6 all-to-all-start.2
  180.3 0.6 multiply_reduce_fusion.48
  182.1 4.6 collective-permute-start.3
  186.7 1.9 collective-permute-start.2
  188.9 690.7 %psum.7 = f32[7,7,128]{2,1,0:T(8,128)S(1)} all-reduce(f32[7,7,128]{2,1,0:T(8,128)S(1)} %constant_dynamic-update-slice_fusion), channel_id=1, replica_groups=mesh['row'=128,'ch'=4] {'row'}, use_global_device_ids=true, to_apply=%region_49.50 | all-reduce | flops 6272 | bytes 50176 | tf_op jit(solution)/shard_map/psum | solution.py:132
  879.6 48.2 %all-to-all-start.3 = ((f32[384,1,128]{2,1,0:T(1,128)}), f32[384,1,128]{2,1,0:T(1,128)S(1)}, u32[]{:S(2)}, u32[]{:S(2)}) async-start(f32[384,1,128]{2,1,0:T(1,128)} %bitcast.67), calls=%async_computation.3 | async-start | bytes 393216 | tf_op jit(solution)/shard_map/all_to_all | solution.py:103
  927.8 0.6 broadcast_multiply_fusion
  928.4 0.6 fusion.150
  929.0 9.5 %all-to-all-done.3 = f32[384,1,128]{2,1,0:T(1,128)S(1)} async-done(((f32[384,1,128]{2,1,0:T(1,128)}), f32[384,1,128]{2,1,0:T(1,128)S(1)}, u32[]{:S(2)}, u32[]{:S(2)}) %all-to-all-start.3) | async-done | bytes 196640 | tf_op jit(solution)/shard_map/all_to_all | solution.py:103
  938.5 1.2 fusion.7
  939.8 1.7 fusion.156
  (46 shorter events, 3.0 us)
Async XLA Ops:
  0.6 8.1 copy-start
  0.6 29.4 %collective-permute-start = (bf16[3,128,128]{2,1,0:T(8,128)(2,1)}, bf16[3,128,128]{2,1,0:T(8,128)(2,1)S(1)}, u32[]{:S(2)}, u32[]{:S(2)}) collective-permute-start(bf16[3,128,128]{2,1,0:T(8,128)(2,1)} %param.4), channel_id=1, source_target_pairs={{0,4},{4,8},{8,12},{12,16},{16,20},{20,24},{24,28},{28,32},{32,36}... | collective-permute-start | bytes 294920 | tf_op jit(solution)/shard_map/ppermute | solution.py:16
  4.2 25.9 %collective-permute-start.1 = (bf16[3,128,128]{2,1,0:T(8,128)(2,1)}, bf16[3,128,128]{2,1,0:T(8,128)(2,1)S(1)}, u32[]{:S(2)}, u32[]{:S(2)}) collective-permute-start(bf16[3,128,128]{2,1,0:T(8,128)(2,1)} %param.4), channel_id=1, source_target_pairs={{4,0},{8,4},{12,8},{16,12},{20,16},{24,20},{28,24},{32,28},{36,32}... | collective-permute-start | bytes 294920 | tf_op jit(solution)/shard_map/ppermute | solution.py:19
  10.1 18.6 %copy-start.2 = (f32[7,7,128]{2,1,0:T(8,128)S(1)}, f32[7,7,128]{2,1,0:T(8,128)}, u32[]{:S(2)}) copy-start(f32[7,7,128]{2,1,0:T(8,128)} %param.5) | copy-start | bytes 75268
  10.1 30.5 %all-to-all-start.5 = ((f32[3,128,128]{2,0,1:T(4,128)}), f32[3,128,128]{2,0,1:T(4,128)S(1)}, u32[]{:S(2)}, u32[]{:S(2)}) async-start(f32[3,128,128]{2,0,1:T(4,128)} %copy.29), calls=%async_computation.5 | async-start | bytes 524288 | tf_op jit(solution)/shard_map/all_to_all | solution.py:107
  29.2 0.9 copy-start.1
  40.6 20.2 %all-to-all-start.4 = ((f32[3,128,128]{2,0,1:T(4,128)}), f32[3,128,128]{2,0,1:T(4,128)S(1)}, u32[]{:S(2)}, u32[]{:S(2)}) async-start(f32[3,128,128]{2,0,1:T(4,128)} %copy.28), calls=%async_computation.4 | async-start | bytes 524288 | tf_op jit(solution)/shard_map/all_to_all | solution.py:106
  60.8 26.5 %all-to-all-start = ((f32[3,128,128]{2,0,1:T(4,128)}), f32[3,128,128]{2,0,1:T(4,128)S(1)}, u32[]{:S(2)}, u32[]{:S(2)}) async-start(f32[3,128,128]{2,0,1:T(4,128)} %copy.22), calls=%async_computation | async-start | bytes 524288 | tf_op jit(solution)/shard_map/all_to_all | solution.py:94
  77.1 3.6 copy-start.3
  87.3 25.9 %all-to-all-start.1 = ((f32[3,128,128]{2,0,1:T(4,128)}), f32[3,128,128]{2,0,1:T(4,128)S(1)}, u32[]{:S(2)}, u32[]{:S(2)}) async-start(f32[3,128,128]{2,0,1:T(4,128)} %copy.23), calls=%async_computation.1 | async-start | bytes 524288 | tf_op jit(solution)/shard_map/all_to_all | solution.py:95
  113.2 33.6 %all-to-all-start.6 = ((f32[384,1,128]{2,1,0:T(1,128)}), f32[384,1,128]{2,1,0:T(1,128)S(1)}, u32[]{:S(2)}, u32[]{:S(2)}) async-start(f32[384,1,128]{2,1,0:T(1,128)} %bitcast.79), calls=%async_computation.6 | async-start | bytes 393216 | tf_op jit(solution)/shard_map/all_to_all | solution.py:116
  146.8 24.9 %all-to-all-start.7 = ((f32[384,1,128]{2,1,0:T(1,128)}), f32[384,1,128]{2,1,0:T(1,128)S(1)}, u32[]{:S(2)}, u32[]{:S(2)}) async-start(f32[384,1,128]{2,1,0:T(1,128)} %bitcast.84), calls=%async_computation.7 | async-start | bytes 393216 | tf_op jit(solution)/shard_map/all_to_all | solution.py:117
  171.7 707.8 %all-to-all-start.2 = ((f32[384,1,128]{2,1,0:T(1,128)}), f32[384,1,128]{2,1,0:T(1,128)S(1)}, u32[]{:S(2)}, u32[]{:S(2)}) async-start(f32[384,1,128]{2,1,0:T(1,128)} %bitcast.62), calls=%async_computation.2 | async-start | bytes 393216 | tf_op jit(solution)/shard_map/all_to_all | solution.py:102
  182.1 757.6 %collective-permute-start.3 = (f32[3,128,128]{2,1,0:T(8,128)S(1)}, f32[3,128,128]{2,1,0:T(8,128)S(1)}, u32[]{:S(2)}, u32[]{:S(2)}) collective-permute-start(f32[3,128,128]{2,1,0:T(8,128)S(1)} %get-tuple-element.116), channel_id=1, source_target_pairs={{4,0},{8,4},{12,8},{16,12},{20,16},{24,20},{28,24},{32,28},{36,32}... | collective-permute-start | bytes 589832 | tf_op jit(solution)/shard_map/ppermute | solution.py:19
  186.7 753.0 %collective-permute-start.2 = (f32[3,128,128]{2,1,0:T(8,128)S(1)}, f32[3,128,128]{2,1,0:T(8,128)S(1)}, u32[]{:S(2)}, u32[]{:S(2)}) collective-permute-start(f32[3,128,128]{2,1,0:T(8,128)S(1)} %get-tuple-element.116), channel_id=1, source_target_pairs={{0,4},{4,8},{8,12},{12,16},{16,20},{20,24},{24,28},{28,32},{32,36}... | collective-permute-start | bytes 589832 | tf_op jit(solution)/shard_map/ppermute | solution.py:16
  879.6 58.9 %all-to-all-start.3 = ((f32[384,1,128]{2,1,0:T(1,128)}), f32[384,1,128]{2,1,0:T(1,128)S(1)}, u32[]{:S(2)}, u32[]{:S(2)}) async-start(f32[384,1,128]{2,1,0:T(1,128)} %bitcast.67), calls=%async_computation.3 | async-start | bytes 393216 | tf_op jit(solution)/shard_map/all_to_all | solution.py:103
where the time goes:
time: 950 us; the launch traced here: 942 us
  blocking collectives  691 us (73%)
  starting transfers between devices  145 us (15%)
  matrix products  60.3 us (6%)
  waiting for transfers between devices  34.8 us (4%)
    psum x1, blocking collectives, row_tiles(): conv_grad = lax.psum(partial_grad, 'row') / math.sqrt(height * col_count)  691 us
    dot_general x16, matrix products, along_rows(): return jnp.einsum('kh,hlc->klc', table, field, precision=HIGHEST)  55.3 us
    all_to_all x1, starting transfers between devices, row_tiles(): lax.all_to_all(inv_im, 'row', split_axis=0, concat_axis=1, tiled=True)  48.2 us
  transfers between devices with their start and end apart: 12, of which 5 were waited for; matrix products, arithmetic and copies ran while one was open for 7% of the time, Pallas kernels for 0%

commit v1 on v0

v1 whole, which is shorter than its diff:
```python
import functools
import math

import jax
import jax.numpy as jnp
import ml_dtypes
import numpy as np
from jax import lax
from jax.experimental import pallas as pl
from jax.experimental.pallas import tpu as pltpu
from jax.sharding import PartitionSpec as P

F32 = jnp.float32
BF16 = jnp.bfloat16
ROWS = 3
SLOT = 8
USED = 6
DEPTH = 8
EDGE = 8
CHUNK = 32


def halves(table):
    high = table.astype(ml_dtypes.bfloat16)
    low = (table - high.astype(np.float64)).astype(ml_dtypes.bfloat16)
    return high, low


def tables(count):
    height = ROWS * count
    index = np.arange(count)
    angle = 2.0 * math.pi * (index[:, None] * index[None, :] % count) / count
    cols = np.zeros((count, SLOT, ROWS, count))
    for row in range(ROWS):
        cols[:, row, row, :] = np.cos(angle)
        cols[:, ROWS + row, row, :] = -np.sin(angle)
    cols = cols.reshape(count * SLOT, ROWS * count)
    index = np.arange(height)
    angle = 2.0 * math.pi * (index[:, None] * index[None, :] % height) / height
    cosine = np.cos(angle).reshape(height, count, ROWS)
    sine = np.sin(angle).reshape(height, count, ROWS)
    rows = np.zeros((2, height, count, SLOT))
    rows[0, :, :, :ROWS], rows[0, :, :, ROWS:USED] = cosine, sine
    rows[1, :, :, :ROWS], rows[1, :, :, ROWS:USED] = -sine, cosine
    rows = rows.reshape(2 * height, count * SLOT)
    one = rows.astype(ml_dtypes.bfloat16)
    return halves(cols) + (one, np.ascontiguousarray(one.T)) + halves(np.ascontiguousarray(cols.T))


def dot(table, value):
    return jnp.dot(table, value, preferred_element_type=F32)


def kernel(
    count,
    tok_hbm, weight_hbm, filt_hbm, cot_hbm, c1h_hbm, c1l_hbm, r2_hbm, r3_hbm, c4h_hbm, c4l_hbm,
    filtered_ref, token_grad_ref, filter_grad_ref, conv_grad_ref,
    tok, weight, filt, cot, c1h, c1l, r2, r3, c4h, c4l,
    send, recv, low_rim, high_rim, tile, field, taps, cot_spec, spec,
    part, by_depth, by_plane, summed, load_sem, send_sem, recv_sem, rim_send, rim_recv, sum_send, sum_recv,
):
    me = lax.axis_index("row")
    height = ROWS * count
    plane = count // DEPTH
    depth_at, plane_at = me // plane, lax.rem(me, plane)
    inverse = 1.0 / (height * count)

    loads = [
        pltpu.make_async_copy(source, target, load_sem.at[i])
        for i, (source, target) in enumerate(
            (
                (cot_hbm, cot), (c1h_hbm, c1h), (c1l_hbm, c1l), (tok_hbm, tok), (weight_hbm, weight),
                (filt_hbm, filt), (r2_hbm, r2), (r3_hbm, r3), (c4h_hbm, c4h), (c4l_hbm, c4l),
            )
        )
    ]
    for load in loads:
        load.start()

    barrier = pltpu.get_barrier_semaphore()

    @pl.loop(1, count)
    def _(i):
        pl.semaphore_signal(barrier, 1, device_id={"row": lax.rem(me + i, count)})

    def scatter(slot):
        @pl.loop(1, count)
        def _(i):
            target = lax.rem(me + i, count)
            pltpu.make_async_remote_copy(
                send.at[slot, target, pl.ds(0, USED)],
                recv.at[slot, me, pl.ds(0, USED)],
                send_sem.at[slot],
                recv_sem.at[slot],
                device_id={"row": target},
            ).start()

        recv[slot, pl.ds(me, 1)] = send[slot, pl.ds(me, 1)]

    def all_of(slot):
        return pltpu.make_async_remote_copy(
            send.at[slot, pl.ds(0, count - 1), pl.ds(0, USED)],
            recv.at[slot, pl.ds(0, count - 1), pl.ds(0, USED)],
            send_sem.at[slot],
            recv_sem.at[slot],
            device_id={"row": lax.rem(me + 1, count)},
        )

    def gathered(slot):
        all_of(slot).wait_recv()
        value = recv[slot].astype(F32)
        row = lax.broadcasted_iota(jnp.int32, value.shape, 1)
        return jnp.where(row < USED, value, 0.0).reshape(count * SLOT, 128).astype(BF16)

    def stage(slot, value):
        send[slot] = value.reshape(count, SLOT, 128).astype(BF16)

    for load in loads[:3]:
        load.wait()
    value = cot[...].reshape(ROWS * count, 128)
    stage(0, dot(c1h[...], value) + dot(c1l[...], value))

    side = jnp.zeros((3 * ROWS, EDGE, 128), F32)
    for ref in (tile, field):
        ref[:, 0:EDGE] = side
        ref[:, EDGE + count : 2 * EDGE + count] = side
    loads[3].wait()
    loads[4].wait()
    tile[ROWS : 2 * ROWS, EDGE : EDGE + count] = tok[...].astype(F32)
    for tap in range(49):
        taps[tap] = jnp.broadcast_to(weight[tap // 7, tap % 7 : tap % 7 + 1, :], (8, 128))
    part[...] = jnp.zeros_like(part)
    no_rim = jnp.zeros((ROWS, count, 128), F32)

    @pl.when(me == 0)
    def _():
        tile[0:ROWS, EDGE : EDGE + count] = no_rim
        field[0:ROWS, EDGE : EDGE + count] = no_rim

    @pl.when(me == count - 1)
    def _():
        tile[2 * ROWS : 3 * ROWS, EDGE : EDGE + count] = no_rim
        field[2 * ROWS : 3 * ROWS, EDGE : EDGE + count] = no_rim

    pl.semaphore_wait(barrier, count - 1)
    scatter(0)

    inner = pl.ds(EDGE, count)
    up, down = {"row": lax.rem(me + 1, count)}, {"row": lax.rem(me + count - 1, count)}
    tok_up = pltpu.make_async_remote_copy(tok, low_rim, rim_send.at[0], rim_recv.at[0], device_id=up)
    tok_down = pltpu.make_async_remote_copy(tok, high_rim, rim_send.at[1], rim_recv.at[1], device_id=down)
    own = field.at[pl.ds(ROWS, ROWS), inner]
    field_up = pltpu.make_async_remote_copy(
        own, field.at[pl.ds(0, ROWS), inner], rim_send.at[2], rim_recv.at[2], device_id=up
    )
    field_down = pltpu.make_async_remote_copy(
        own, field.at[pl.ds(2 * ROWS, ROWS), inner], rim_send.at[3], rim_recv.at[3], device_id=down
    )

    def start_rims(to_up, to_down):
        @pl.when(me < count - 1)
        def _():
            to_up.start()

        @pl.when(me > 0)
        def _():
            to_down.start()

    start_rims(tok_up, tok_down)

    def depthwise(source, flip, start):
        total = [jnp.zeros((CHUNK // 8, 8, 128), F32) for _ in range(ROWS)]
        for b in range(7):
            for r in range(3 * ROWS):
                value = source[r, pl.ds(start + (EDGE - 3 + b), CHUNK), :].reshape(CHUNK // 8, 8, 128)
                for j in range(ROWS):
                    a = r - j
                    if 0 <= a < 7:
                        tap = 48 - (a * 7 + b) if flip else a * 7 + b
                        total[j] = total[j] + value * taps[tap]
        return [t.reshape(CHUNK, 128) for t in total]

    @pl.when(me > 0)
    def _():
        tok_up.wait_recv()
        tile[0:ROWS, EDGE : EDGE + count] = low_rim[...].astype(F32)

    @pl.when(me < count - 1)
    def _():
        tok_down.wait_recv()
        tile[2 * ROWS : 3 * ROWS, EDGE : EDGE + count] = high_rim[...].astype(F32)

    @pl.loop(0, count // CHUNK)
    def _(i):
        start = pl.multiple_of(i * CHUNK, CHUNK)
        for j, total in enumerate(depthwise(tile, False, start)):
            spec[pl.ds(pl.multiple_of(j * count + start, CHUNK), CHUNK), :] = total

    value = spec[0 : ROWS * count, :]
    high = value.astype(BF16)
    low = (value - high.astype(F32)).astype(BF16)
    stage(1, dot(c1h[...], high) + (dot(c1l[...], high) + dot(c1h[...], low)))
    scatter(1)

    for load in loads[5:8]:
        load.wait()
    cot_spec[...] = dot(r2[...], gathered(0)) * inverse
    cot_re, cot_im = cot_spec[0:height, :], cot_spec[height : 2 * height, :]
    filt_re, filt_im = filt[0].astype(F32), filt[1].astype(F32)
    back = jnp.concatenate(
        [(cot_re * filt_re + cot_im * filt_im).astype(BF16), (cot_im * filt_re - cot_re * filt_im).astype(BF16)]
    )
    stage(2, dot(r3[...], back))
    scatter(2)

    spec[...] = dot(r2[...], gathered(1))
    spec_re, spec_im = spec[0:height, :], spec[height : 2 * height, :]
    filt_re, filt_im = filt[0].astype(F32), filt[1].astype(F32)
    product = jnp.concatenate(
        [
            (filt_re * spec_re - filt_im * spec_im).astype(BF16),
            (filt_re * spec_im + filt_im * spec_re).astype(BF16),
        ]
    )
    stage(3, dot(r3[...], product))
    scatter(3)
    cot_re, cot_im = cot_spec[0:height, :], cot_spec[height : 2 * height, :]
    spec_re, spec_im = spec[0:height, :], spec[height : 2 * height, :]
    filter_grad_ref[0] = cot_re * spec_re + cot_im * spec_im
    filter_grad_ref[1] = cot_im * spec_re - cot_re * spec_im

    loads[8].wait()
    loads[9].wait()
    value = gathered(2)
    field[ROWS : 2 * ROWS, EDGE : EDGE + count] = (dot(c4h[...], value) + dot(c4l[...], value)).reshape(ROWS, count, 128)

    @pl.loop(0, 7)
    def _(b):
        total = [jnp.zeros((8, 128), F32) for _ in range(7)]
        for i in range(count // CHUNK):
            grads = [
                field[ROWS + j, EDGE + i * CHUNK : EDGE + (i + 1) * CHUNK, :].reshape(CHUNK // 8, 8, 128)
                for j in range(ROWS)
            ]
            for r in range(3 * ROWS):
                value = tile[r, pl.ds(i * CHUNK + EDGE - 3 + b, CHUNK), :].reshape(CHUNK // 8, 8, 128)
                for j in range(ROWS):
                    if 0 <= r - j < 7:
                        total[r - j] = total[r - j] + jnp.sum(grads[j] * value, axis=0)
        for a in range(7):
            part[a, pl.ds(b, 1), :] = jnp.sum(total[a], axis=0, keepdims=True)

    def depth_peer(i):
        return lax.rem(depth_at + i, DEPTH)

    for i in range(1, DEPTH):
        peer = depth_peer(i)
        pltpu.make_async_remote_copy(
            part.at[peer], by_depth.at[i], sum_send.at[0], sum_recv.at[0], device_id={"row": peer * plane + plane_at}
        ).start()
    start_rims(field_up, field_down)

    value = gathered(3)
    filtered_ref[...] = (
        ((dot(c4h[...], value) + dot(c4l[...], value)) * inverse).reshape(ROWS, count, 128).astype(BF16)
    )

    def sums(source, target, stage_at):
        return pltpu.make_async_remote_copy(
            source, target, sum_send.at[stage_at], sum_recv.at[stage_at], device_id=up
        )

    others = pl.ds(1, DEPTH - 1)
    plane_others = pl.ds(0, plane - 1)
    sums(part.at[others], by_depth.at[others], 0).wait_recv()
    total = part[depth_at]
    for i in range(1, DEPTH):
        total = total + by_depth[i]
    by_plane[plane_at] = total

    @pl.loop(1, plane)
    def _(i):
        peer = lax.rem(plane_at + i, plane)
        pltpu.make_async_remote_copy(
            by_plane.at[plane_at], by_plane.at[plane_at], sum_send.at[1], sum_recv.at[1],
            device_id={"row": depth_at * plane + peer},
        ).start()

    @pl.when(me > 0)
    def _():
        field_up.wait_recv()

    @pl.when(me < count - 1)
    def _():
        field_down.wait_recv()

    @pl.loop(0, count // CHUNK)
    def _(i):
        start = pl.multiple_of(i * CHUNK, CHUNK)
        for j, total in enumerate(depthwise(field, True, start)):
            token_grad_ref[j, pl.ds(start, CHUNK), :] = total.astype(BF16)

    sums(by_plane.at[plane_others], by_plane.at[plane_others], 1).wait_recv()
    total = by_plane[0]
    for i in range(1, plane):
        total = total + by_plane[i]
    summed[depth_at] = total * (1.0 / math.sqrt(height * count))
    for i in range(1, DEPTH):
        pltpu.make_async_remote_copy(
            summed.at[depth_at], summed.at[depth_at], sum_send.at[2], sum_recv.at[2],
            device_id={"row": depth_peer(i) * plane + plane_at},
        ).start()
    sums(summed.at[others], summed.at[others], 2).wait_recv()
    for a in range(7):
        conv_grad_ref[a] = summed[a, 0:7, :]

    for slot in range(4):
        all_of(slot).wait_send()

    @pl.when(me < count - 1)
    def _():
        tok_up.wait_send()
        field_up.wait_send()

    @pl.when(me > 0)
    def _():
        tok_down.wait_send()
        field_down.wait_send()

    sums(part.at[others], by_depth.at[others], 0).wait_send()
    sums(by_plane.at[plane_others], by_plane.at[plane_others], 1).wait_send()
    sums(summed.at[others], summed.at[others], 2).wait_send()


def per_device(constants, tokens, conv_weight, spectral_filter, cotangent):
    rows, count, lanes = tokens.shape
    height = rows * count
    plane = count // DEPTH
    vmem = pltpu.VMEM
    dma = pltpu.SemaphoreType.DMA
    loaded = [tokens, conv_weight, spectral_filter.reshape(2, height, lanes), cotangent, *constants]
    filtered, token_grad, filter_grad, conv_grad = pl.pallas_call(
        functools.partial(kernel, count),
        out_shape=(
            jax.ShapeDtypeStruct((rows, count, lanes), BF16),
            jax.ShapeDtypeStruct((rows, count, lanes), BF16),
            jax.ShapeDtypeStruct((2, height, lanes), F32),
            jax.ShapeDtypeStruct((7, 7, lanes), F32),
        ),
        in_specs=[pl.BlockSpec(memory_space=pl.ANY)] * len(loaded),
        out_specs=(pl.BlockSpec(memory_space=pltpu.VMEM),) * 4,
        scratch_shapes=[vmem(x.shape, x.dtype) for x in loaded]
        + [
            vmem((4, count, SLOT, lanes), BF16),
            vmem((4, count, SLOT, lanes), BF16),
            vmem((rows, count, lanes), BF16),
            vmem((rows, count, lanes), BF16),
            vmem((3 * rows, count + 2 * EDGE, lanes), F32),
            vmem((3 * rows, count + 2 * EDGE, lanes), F32),
            vmem((49, 8, lanes), F32),
            vmem((2 * height, lanes), F32),
            vmem((2 * height, lanes), F32),
            vmem((DEPTH, 8, lanes), F32),
            vmem((DEPTH, 8, lanes), F32),
            vmem((plane, 8, lanes), F32),
            vmem((DEPTH, 8, lanes), F32),
            dma((len(loaded),)),
            dma((4,)),
            dma((4,)),
            dma((4,)),
            dma((4,)),
            dma((3,)),
            dma((3,)),
        ],
        name="global_filter",
        compiler_params=pltpu.CompilerParams(collective_id=0, has_side_effects=True),
    )(*loaded)
    return filtered, token_grad, filter_grad.reshape(2, height, 1, lanes), conv_grad


def solution(mesh):
    constants = [jnp.asarray(table) for table in tables(mesh.shape["row"])]
    return jax.shard_map(
        functools.partial(per_device, constants),
        mesh=mesh,
        in_specs=(P("row", None, "ch"), P(None, None, "ch"), P(None, None, "row", "ch"), P("row", None, "ch")),
        out_specs=(P("row", None, "ch"), P("row", None, "ch"), P(None, None, "row", "ch"), P(None, None, "ch")),
        check_vma=False,
    )
```

time: 950 us -> 69 us (0.07)
  blocking collectives: 691 us -> 0 us
  starting transfers between devices: 145 us -> 0 us
  Pallas kernels: 0 us -> 61.6 us
  matrix products: 60.3 us -> 0 us
  waiting for transfers between devices: 34.8 us -> 0 us
    psum x1 -> x0, blocking collectives: 691 us -> none  [row_tiles(): conv_grad = lax.psum(partial_grad, 'row') / math.sqrt(height * col_count)]
    all_to_all x8 -> x0, starting transfers between devices: 131 us -> none  [the longest x1 48.2 us: row_tiles(): lax.all_to_all(inv_im, 'row', split_axis=0, concat_axis=1, tiled=True)]
    pallas_call x0 -> x1, Pallas kernels: none -> 61.6 us  [per_device(): pl.pallas_call(functools.partial(kernel, count), out_shape=(jax.ShapeDtyp...]
    dot_general x24 -> x0, matrix products: 60.3 us -> none  [the longest x16 55.3 us: along_rows(): return jnp.einsum('kh,hlc->klc', table, field, precision=HIGHEST)]
    all_to_all x8 -> x0, waiting for transfers between devices: 34.7 us -> none  [the longest x1 9.53 us: row_tiles(): lax.all_to_all(inv_im, 'row', split_axis=0, concat_axis=1, tiled=True)]
    ppermute x4 -> x0, starting transfers between devices: 14.6 us -> none  [the longest x2 9.13 us: extended(): lax.ppermute(lax.slice_in_dim(block, 0, width, axis=dim), axis, backward)]
  transfers between devices with their start and end apart: 12 -> 0, of which waited for: 5 -> 0; matrix products, arithmetic and copies ran while one was open for 7% -> 0% of each run, Pallas kernels for 0% -> 0%
where the time goes in v1:
time: 69 us; the launch traced here: 68.4 us
  Pallas kernels  61.6 us (89%)
  local copies, waits for them, and re-layouts  6.2 us (9%)
    pallas_call x1, Pallas kernels, per_device(): pl.pallas_call(functools.partial(kernel, count), out_shape=(jax.ShapeDtyp...  61.6 us
    unnamed x4, local copies, waits for them, and re-layouts  6.2 us

profile of v1, /device:TPU:56, one launch (start us, length us, event | category | flops | bytes accessed | tf_op | source)
XLA Modules:
  0.0 68.4 jit_solution(15260550181789727830)
XLA Ops:
  0.6 61.6 %global_filter.1 = (bf16[3,128,128]{2,1,0:T(8,128)(2,1)}, bf16[3,128,128]{2,1,0:T(8,128)(2,1)}, f32[2,384,128]{2,1,0:T(8,128)}, f32[7,7,128]{2,1,0:T(8,128)}) custom-call(bf16[3,128,128]{2,1,0:T(8,128)(2,1)} %tok_hbm.1, f32[7,7,128]{2,1,0:T(8,128)} %weight_hbm.1, bf16[2,384,128]{2,1,0:T(8,128)(2,1)} %bitcast.5, bf16[3,128,128]{2,1,0:T(8,128)(2,1)} %cot_hbm.1, ...), custom_call_target="tpu_custom_call" | custom-call | tf_op jit(solution)/shard_map/global_filter/pallas_call | solution.py:342
  62.2 1.5 %copy.19 = bf16[3,128,128]{2,1,0:T(8,128)(2,1)} copy(bf16[3,128,128]{2,1,0:T(8,128)(2,1)} %get-tuple-element.20) | data formatting | bytes 196608
  63.8 1.5 %copy.20 = bf16[3,128,128]{2,1,0:T(8,128)(2,1)} copy(bf16[3,128,128]{2,1,0:T(8,128)(2,1)} %get-tuple-element.21) | data formatting | bytes 196608
  65.3 1.8 %copy.21 = f32[2,384,1,128]{3,2,1,0:T(1,128)} copy(f32[2,384,1,128]{3,2,1,0:T(1,128)} %bitcast.4) | data formatting | bytes 786432
  67.1 1.4 %copy.22 = f32[7,7,128]{2,1,0:T(8,128)} copy(f32[7,7,128]{2,1,0:T(8,128)} %get-tuple-element.23) | data formatting | bytes 50176

commit v2 on v1

--- a/solution.py
+++ b/solution.py
@@ -18,6 +18,8 @@
 DEPTH = 8
 EDGE = 8
 CHUNK = 32
+QUARTERS = 4
+ORDER = (2, 1, 3, 0)
 
 
 def halves(table):
@@ -62,7 +64,7 @@
     me = lax.axis_index("row")
     height = ROWS * count
     plane = count // DEPTH
-    depth_at, plane_at = me // plane, lax.rem(me, plane)
+    depth_at, plane_at = me // plane, jnp.bitwise_and(me, plane - 1)
     inverse = 1.0 / (height * count)
 
     loads = [
@@ -79,22 +81,38 @@
 
     barrier = pltpu.get_barrier_semaphore()
 
-    @pl.loop(1, count)
-    def _(i):
-        pl.semaphore_signal(barrier, 1, device_id={"row": lax.rem(me + i, count)})
-
-    def scatter(slot):
-        @pl.loop(1, count)
-        def _(i):
-            target = lax.rem(me + i, count)
-            pltpu.make_async_remote_copy(
-                send.at[slot, target, pl.ds(0, USED)],
-                recv.at[slot, me, pl.ds(0, USED)],
-                send_sem.at[slot],
-                recv_sem.at[slot],
-                device_id={"row": target},
-            ).start()
-
+    quarter = count // QUARTERS
+    home = me // quarter
+
+    def peers(shift):
+        base = jnp.bitwise_and(home + shift, QUARTERS - 1) * quarter
+        for i in range(1 if shift == 0 else 0, quarter):
+            yield base + jnp.bitwise_and(me + i, quarter - 1)
+
+    for shift in ORDER:
+        for target in peers(shift):
+            pl.semaphore_signal(barrier, 1, device_id={"row": target})
+
+    def scatter(slot, table_parts, wait=None):
+        for shift in ORDER:
+            base = jnp.bitwise_and(home + shift, QUARTERS - 1)
+            rows = pl.ds(pl.multiple_of(base * (quarter * SLOT), quarter * SLOT), quarter * SLOT)
+            total = None
+            for table, value in table_parts:
+                term = dot(table[rows, :], value)
+                total = term if total is None else total + term
+            send[slot, pl.ds(base * quarter, quarter)] = total.reshape(quarter, SLOT, 128).astype(BF16)
+            if wait is not None:
+                wait()
+                wait = None
+            for target in peers(shift):
+                pltpu.make_async_remote_copy(
+                    send.at[slot, target, pl.ds(0, USED)],
+                    recv.at[slot, me, pl.ds(0, USED)],
+                    send_sem.at[slot],
+                    recv_sem.at[slot],
+                    device_id={"row": target},
+                ).start()
         recv[slot, pl.ds(me, 1)] = send[slot, pl.ds(me, 1)]
 
     def all_of(slot):
@@ -103,7 +121,7 @@
             recv.at[slot, pl.ds(0, count - 1), pl.ds(0, USED)],
             send_sem.at[slot],
             recv_sem.at[slot],
-            device_id={"row": lax.rem(me + 1, count)},
+            device_id={"row": jnp.bitwise_and(me + 1, count - 1)},
         )
 
     def gathered(slot):
@@ -111,14 +129,6 @@
         value = recv[slot].astype(F32)
         row = lax.broadcasted_iota(jnp.int32, value.shape, 1)
         return jnp.where(row < USED, value, 0.0).reshape(count * SLOT, 128).astype(BF16)
-
-    def stage(slot, value):
-        send[slot] = value.reshape(count, SLOT, 128).astype(BF16)
-
-    for load in loads[:3]:
-        load.wait()
-    value = cot[...].reshape(ROWS * count, 128)
-    stage(0, dot(c1h[...], value) + dot(c1l[...], value))
 
     side = jnp.zeros((3 * ROWS, EDGE, 128), F32)
     for ref in (tile, field):
@@ -142,11 +152,13 @@
         tile[2 * ROWS : 3 * ROWS, EDGE : EDGE + count] = no_rim
         field[2 * ROWS : 3 * ROWS, EDGE : EDGE + count] = no_rim
 
-    pl.semaphore_wait(barrier, count - 1)
-    scatter(0)
+    for load in loads[:3]:
+        load.wait()
+    value = cot[...].reshape(ROWS * count, 128)
+    scatter(0, ((c1h, value), (c1l, value)), lambda: pl.semaphore_wait(barrier, count - 1))
 
     inner = pl.ds(EDGE, count)
-    up, down = {"row": lax.rem(me + 1, count)}, {"row": lax.rem(me + count - 1, count)}
+    up, down = {"row": jnp.bitwise_and(me + 1, count - 1)}, {"row": jnp.bitwise_and(me + count - 1, count - 1)}
     tok_up = pltpu.make_async_remote_copy(tok, low_rim, rim_send.at[0], rim_recv.at[0], device_id=up)
     tok_down = pltpu.make_async_remote_copy(tok, high_rim, rim_send.at[1], rim_recv.at[1], device_id=down)
     own = field.at[pl.ds(ROWS, ROWS), inner]
@@ -199,8 +211,7 @@
     value = spec[0 : ROWS * count, :]
     high = value.astype(BF16)
     low = (value - high.astype(F32)).astype(BF16)
-    stage(1, dot(c1h[...], high) + (dot(c1l[...], high) + dot(c1h[...], low)))
-    scatter(1)
+    scatter(1, ((c1h, high), (c1l, high), (c1h, low)))
 
     for load in loads[5:8]:
         load.wait()
@@ -210,8 +221,7 @@
     back = jnp.concatenate(
         [(cot_re * filt_re + cot_im * filt_im).astype(BF16), (cot_im * filt_re - cot_re * filt_im).astype(BF16)]
     )
-    stage(2, dot(r3[...], back))
-    scatter(2)
+    scatter(2, ((r3, back),))
 
     spec[...] = dot(r2[...], gathered(1))
     spec_re, spec_im = spec[0:height, :], spec[height : 2 * height, :]
@@ -222,8 +232,7 @@
             (filt_re * spec_im + filt_im * spec_re).astype(BF16),
         ]
     )
-    stage(3, dot(r3[...], product))
-    scatter(3)
+    scatter(3, ((r3, product),))
     cot_re, cot_im = cot_spec[0:height, :], cot_spec[height : 2 * height, :]
     spec_re, spec_im = spec[0:height, :], spec[height : 2 * height, :]
     filter_grad_ref[0] = cot_re * spec_re + cot_im * spec_im
@@ -251,7 +260,7 @@
             part[a, pl.ds(b, 1), :] = jnp.sum(total[a], axis=0, keepdims=True)
 
     def depth_peer(i):
-        return lax.rem(depth_at + i, DEPTH)
+        return jnp.bitwise_and(depth_at + i, DEPTH - 1)
 
     for i in range(1, DEPTH):
         peer = depth_peer(i)
@@ -259,11 +268,6 @@
             part.at[peer], by_depth.at[i], sum_send.at[0], sum_recv.at[0], device_id={"row": peer * plane + plane_at}
         ).start()
     start_rims(field_up, field_down)
-
-    value = gathered(3)
-    filtered_ref[...] = (
-        ((dot(c4h[...], value) + dot(c4l[...], value)) * inverse).reshape(ROWS, count, 128).astype(BF16)
-    )
 
     def sums(source, target, stage_at):
         return pltpu.make_async_remote_copy(
@@ -278,27 +282,17 @@
         total = total + by_depth[i]
     by_plane[plane_at] = total
 
-    @pl.loop(1, plane)
-    def _(i):
-        peer = lax.rem(plane_at + i, plane)
+    for i in range(1, plane):
+        peer = jnp.bitwise_and(plane_at + i, plane - 1)
         pltpu.make_async_remote_copy(
             by_plane.at[plane_at], by_plane.at[plane_at], sum_send.at[1], sum_recv.at[1],
             device_id={"row": depth_at * plane + peer},
         ).start()
 
-    @pl.when(me > 0)
-    def _():
-        field_up.wait_recv()
-
-    @pl.when(me < count - 1)
-    def _():
-        field_down.wait_recv()
-
-    @pl.loop(0, count // CHUNK)
-    def _(i):
-        start = pl.multiple_of(i * CHUNK, CHUNK)
-        for j, total in enumerate(depthwise(field, True, start)):
-            token_grad_ref[j, pl.ds(start, CHUNK), :] = total.astype(BF16)
+    value = gathered(3)
+    filtered_ref[...] = (
+        ((dot(c4h[...], value) + dot(c4l[...], value)) * inverse).reshape(ROWS, count, 128).astype(BF16)
+    )
 
     sums(by_plane.at[plane_others], by_plane.at[plane_others], 1).wait_recv()
     total = by_plane[0]
@@ -310,6 +304,20 @@
             summed.at[depth_at], summed.at[depth_at], sum_send.at[2], sum_recv.at[2],
             device_id={"row": depth_peer(i) * plane + plane_at},
         ).start()
+    @pl.when(me > 0)
+    def _():
+        field_up.wait_recv()
+
+    @pl.when(me < count - 1)
+    def _():
+        field_down.wait_recv()
+
+    @pl.loop(0, count // CHUNK)
+    def _(i):
+        start = pl.multiple_of(i * CHUNK, CHUNK)
+        for j, total in enumerate(depthwise(field, True, start)):
+            token_grad_ref[j, pl.ds(start, CHUNK), :] = total.astype(BF16)
+
     sums(summed.at[others], summed.at[others], 2).wait_recv()
     for a in range(7):
         conv_grad_ref[a] = summed[a, 0:7, :]
@@ -330,6 +338,15 @@
     sums(part.at[others], by_depth.at[others], 0).wait_send()
     sums(by_plane.at[plane_others], by_plane.at[plane_others], 1).wait_send()
     sums(summed.at[others], summed.at[others], 2).wait_send()
+
+
+def deliver(*refs):
+    sources, targets, sems = refs[:4], refs[4:8], refs[8]
+    copies = [pltpu.make_async_copy(s, t, sems.at[i]) for i, (s, t) in enumerate(zip(sources, targets))]
+    for copy in copies:
+        copy.start()
+    for copy in copies:
+        copy.wait()
 
 
 def per_device(constants, tokens, conv_weight, spectral_filter, cotangent):
@@ -339,14 +356,15 @@
     vmem = pltpu.VMEM
     dma = pltpu.SemaphoreType.DMA
     loaded = [tokens, conv_weight, spectral_filter.reshape(2, height, lanes), cotangent, *constants]
-    filtered, token_grad, filter_grad, conv_grad = pl.pallas_call(
+    shapes = (
+        ((rows, count, lanes), BF16),
+        ((rows, count, lanes), BF16),
+        ((2, height, lanes), F32),
+        ((7, 7, lanes), F32),
+    )
+    results = pl.pallas_call(
         functools.partial(kernel, count),
-        out_shape=(
-            jax.ShapeDtypeStruct((rows, count, lanes), BF16),
-            jax.ShapeDtypeStruct((rows, count, lanes), BF16),
-            jax.ShapeDtypeStruct((2, height, lanes), F32),
-            jax.ShapeDtypeStruct((7, 7, lanes), F32),
-        ),
+        out_shape=tuple(pltpu.VMEM(*shape) for shape in shapes),
         in_specs=[pl.BlockSpec(memory_space=pl.ANY)] * len(loaded),
         out_specs=(pl.BlockSpec(memory_space=pltpu.VMEM),) * 4,
         scratch_shapes=[vmem(x.shape, x.dtype) for x in loaded]
@@ -375,6 +393,14 @@
         name="global_filter",
         compiler_params=pltpu.CompilerParams(collective_id=0, has_side_effects=True),
     )(*loaded)
+    filtered, token_grad, filter_grad, conv_grad = pl.pallas_call(
+        deliver,
+        out_shape=tuple(jax.ShapeDtypeStruct(*shape) for shape in shapes),
+        in_specs=[pl.BlockSpec(memory_space=pltpu.VMEM)] * 4,
+        out_specs=(pl.BlockSpec(memory_space=pl.ANY),) * 4,
+        scratch_shapes=[dma((4,))],
+        name="deliver",
+    )(*[pltpu.with_memory_space_constraint(x, pltpu.VMEM) for x in results])
     return filtered, token_grad, filter_grad.reshape(2, height, 1, lanes), conv_grad
 
 

time: 69 us -> 60.4 us (0.88)
  local copies, waits for them, and re-layouts: 6.2 us -> 0 us
  Pallas kernels: 61.6 us -> 59.7 us
    unnamed x4 -> x0, local copies, waits for them, and re-layouts: 6.2 us -> none
    pallas_call x1 -> x2, Pallas kernels: 61.6 us -> 59.7 us  [the longest x1 58.8 us: per_device(): pl.pallas_call(functools.partial(kernel, count), out_shape=tuple((pltpu.V...]
where the time goes in v2:
time: 60.4 us; the launch traced here: 60.3 us
  Pallas kernels  59.7 us (99%)
  between operations  0.64 us (1%)
    pallas_call x1, Pallas kernels, per_device(): pl.pallas_call(functools.partial(kernel, count), out_shape=tuple((pltpu.V...  58.8 us

profile of v2, /device:TPU:56, one launch (start us, length us, event | category | flops | bytes accessed | tf_op | source)
XLA Modules:
  0.0 60.3 jit_solution(2340677321576880990)
XLA Ops:
  0.6 58.8 %global_filter.1 = (bf16[3,128,128]{2,1,0:T(8,128)(2,1)S(1)}, bf16[3,128,128]{2,1,0:T(8,128)(2,1)S(1)}, f32[2,384,128]{2,1,0:T(8,128)S(1)}, f32[7,7,128]{2,1,0:T(8,128)S(1)}) custom-call(bf16[3,128,128]{2,1,0:T(8,128)(2,1)} %tok_hbm.1, f32[7,7,128]{2,1,0:T(8,128)} %weight_hbm.1, bf16[2,384,128]{2,1,0:T(8,128)(2,1)} %bitcast.4, bf16[3,128,128]{2,1,0:T(8,128)(2,1)} %cot_hbm.1, ...), custom_call_target="tpu_custom_call" | custom-call | tf_op jit(solution)/shard_map/global_filter/pallas_call | solution.py:365
  59.5 0.9 %deliver.1 = (bf16[3,128,128]{2,1,0:T(8,128)(2,1)}, bf16[3,128,128]{2,1,0:T(8,128)(2,1)}, f32[2,384,128]{2,1,0:T(8,128)}, f32[7,7,128]{2,1,0:T(8,128)}) custom-call(bf16[3,128,128]{2,1,0:T(8,128)(2,1)S(1)} %get-tuple-element.12.refs_0_, bf16[3,128,128]{2,1,0:T(8,128)(2,1)S(1)} %get-tuple-element.13.refs_1_, f32[2,384,128]{2,1,0:T(8,128)S(1)} %get-tuple-element.14.refs_2_, ...), custom_call_target="tpu_custom_call" | custom-call | tf_op jit(solution)/shard_map/deliver/pallas_call | solution.py:396

commit v3 on v2

--- a/solution.py
+++ b/solution.py
@@ -58,7 +58,7 @@
     tok_hbm, weight_hbm, filt_hbm, cot_hbm, c1h_hbm, c1l_hbm, r2_hbm, r3_hbm, c4h_hbm, c4l_hbm,
     filtered_ref, token_grad_ref, filter_grad_ref, conv_grad_ref,
     tok, weight, filt, cot, c1h, c1l, r2, r3, c4h, c4l,
-    send, recv, low_rim, high_rim, tile, field, taps, cot_spec, spec,
+    send, recv, low_rim, high_rim, edge, low_edge, high_edge, tile, field, taps, cot_spec, spec,
     part, by_depth, by_plane, summed, load_sem, send_sem, recv_sem, rim_send, rim_recv, sum_send, sum_recv,
 ):
     me = lax.axis_index("row")
@@ -152,21 +152,14 @@
         tile[2 * ROWS : 3 * ROWS, EDGE : EDGE + count] = no_rim
         field[2 * ROWS : 3 * ROWS, EDGE : EDGE + count] = no_rim
 
-    for load in loads[:3]:
-        load.wait()
-    value = cot[...].reshape(ROWS * count, 128)
-    scatter(0, ((c1h, value), (c1l, value)), lambda: pl.semaphore_wait(barrier, count - 1))
-
-    inner = pl.ds(EDGE, count)
     up, down = {"row": jnp.bitwise_and(me + 1, count - 1)}, {"row": jnp.bitwise_and(me + count - 1, count - 1)}
     tok_up = pltpu.make_async_remote_copy(tok, low_rim, rim_send.at[0], rim_recv.at[0], device_id=up)
     tok_down = pltpu.make_async_remote_copy(tok, high_rim, rim_send.at[1], rim_recv.at[1], device_id=down)
-    own = field.at[pl.ds(ROWS, ROWS), inner]
     field_up = pltpu.make_async_remote_copy(
-        own, field.at[pl.ds(0, ROWS), inner], rim_send.at[2], rim_recv.at[2], device_id=up
+        edge, low_edge, rim_send.at[2], rim_recv.at[2], device_id=up
     )
     field_down = pltpu.make_async_remote_copy(
-        own, field.at[pl.ds(2 * ROWS, ROWS), inner], rim_send.at[3], rim_recv.at[3], device_id=down
+        edge, high_edge, rim_send.at[3], rim_recv.at[3], device_id=down
     )
 
     def start_rims(to_up, to_down):
@@ -177,8 +170,6 @@
         @pl.when(me > 0)
         def _():
             to_down.start()
-
-    start_rims(tok_up, tok_down)
 
     def depthwise(source, flip, start):
         total = [jnp.zeros((CHUNK // 8, 8, 128), F32) for _ in range(ROWS)]
@@ -192,6 +183,22 @@
                         total[j] = total[j] + value * taps[tap]
         return [t.reshape(CHUNK, 128) for t in total]
 
+    def sums(source, target, stage_at):
+        return pltpu.make_async_remote_copy(
+            source, target, sum_send.at[stage_at], sum_recv.at[stage_at], device_id=up
+        )
+
+    others = pl.ds(1, DEPTH - 1)
+    plane_others = pl.ds(0, plane - 1)
+    def enter():
+        pl.semaphore_wait(barrier, count - 1)
+        start_rims(tok_up, tok_down)
+
+    for load in loads[:3]:
+        load.wait()
+    value = cot[...].reshape(ROWS * count, 128)
+    scatter(0, ((c1h, value), (c1l, value)), enter)
+
     @pl.when(me > 0)
     def _():
         tok_up.wait_recv()
@@ -223,25 +230,12 @@
     )
     scatter(2, ((r3, back),))
 
-    spec[...] = dot(r2[...], gathered(1))
-    spec_re, spec_im = spec[0:height, :], spec[height : 2 * height, :]
-    filt_re, filt_im = filt[0].astype(F32), filt[1].astype(F32)
-    product = jnp.concatenate(
-        [
-            (filt_re * spec_re - filt_im * spec_im).astype(BF16),
-            (filt_re * spec_im + filt_im * spec_re).astype(BF16),
-        ]
-    )
-    scatter(3, ((r3, product),))
-    cot_re, cot_im = cot_spec[0:height, :], cot_spec[height : 2 * height, :]
-    spec_re, spec_im = spec[0:height, :], spec[height : 2 * height, :]
-    filter_grad_ref[0] = cot_re * spec_re + cot_im * spec_im
-    filter_grad_ref[1] = cot_im * spec_re - cot_re * spec_im
-
     loads[8].wait()
     loads[9].wait()
     value = gathered(2)
-    field[ROWS : 2 * ROWS, EDGE : EDGE + count] = (dot(c4h[...], value) + dot(c4l[...], value)).reshape(ROWS, count, 128)
+    grad = (dot(c4h[...], value) + dot(c4l[...], value)).reshape(ROWS, count, 128)
+    field[ROWS : 2 * ROWS, EDGE : EDGE + count] = grad
+    edge[...] = grad.astype(BF16)
 
     @pl.loop(0, 7)
     def _(b):
@@ -267,15 +261,7 @@
         pltpu.make_async_remote_copy(
             part.at[peer], by_depth.at[i], sum_send.at[0], sum_recv.at[0], device_id={"row": peer * plane + plane_at}
         ).start()
-    start_rims(field_up, field_down)
-
-    def sums(source, target, stage_at):
-        return pltpu.make_async_remote_copy(
-            source, target, sum_send.at[stage_at], sum_recv.at[stage_at], device_id=up
-        )
-
-    others = pl.ds(1, DEPTH - 1)
-    plane_others = pl.ds(0, plane - 1)
+
     sums(part.at[others], by_depth.at[others], 0).wait_recv()
     total = part[depth_at]
     for i in range(1, DEPTH):
@@ -289,10 +275,22 @@
             device_id={"row": depth_at * plane + peer},
         ).start()
 
-    value = gathered(3)
-    filtered_ref[...] = (
-        ((dot(c4h[...], value) + dot(c4l[...], value)) * inverse).reshape(ROWS, count, 128).astype(BF16)
-    )
+    start_rims(field_up, field_down)
+
+    spec[...] = dot(r2[...], gathered(1))
+    spec_re, spec_im = spec[0:height, :], spec[height : 2 * height, :]
+    filt_re, filt_im = filt[0].astype(F32), filt[1].astype(F32)
+    product = jnp.concatenate(
+        [
+            (filt_re * spec_re - filt_im * spec_im).astype(BF16),
+            (filt_re * spec_im + filt_im * spec_re).astype(BF16),
+        ]
+    )
+    scatter(3, ((r3, product),))
+    cot_re, cot_im = cot_spec[0:height, :], cot_spec[height : 2 * height, :]
+    spec_re, spec_im = spec[0:height, :], spec[height : 2 * height, :]
+    filter_grad_ref[0] = cot_re * spec_re + cot_im * spec_im
+    filter_grad_ref[1] = cot_im * spec_re - cot_re * spec_im
 
     sums(by_plane.at[plane_others], by_plane.at[plane_others], 1).wait_recv()
     total = by_plane[0]
@@ -307,16 +305,23 @@
     @pl.when(me > 0)
     def _():
         field_up.wait_recv()
+        field[0:ROWS, EDGE : EDGE + count] = low_edge[...].astype(F32)
 
     @pl.when(me < count - 1)
     def _():
         field_down.wait_recv()
+        field[2 * ROWS : 3 * ROWS, EDGE : EDGE + count] = high_edge[...].astype(F32)
 
     @pl.loop(0, count // CHUNK)
     def _(i):
         start = pl.multiple_of(i * CHUNK, CHUNK)
         for j, total in enumerate(depthwise(field, True, start)):
             token_grad_ref[j, pl.ds(start, CHUNK), :] = total.astype(BF16)
+
+    value = gathered(3)
+    filtered_ref[...] = (
+        ((dot(c4h[...], value) + dot(c4l[...], value)) * inverse).reshape(ROWS, count, 128).astype(BF16)
+    )
 
     sums(summed.at[others], summed.at[others], 2).wait_recv()
     for a in range(7):
@@ -371,6 +376,9 @@
         + [
             vmem((4, count, SLOT, lanes), BF16),
             vmem((4, count, SLOT, lanes), BF16),
+            vmem((rows, count, lanes), BF16),
+            vmem((rows, count, lanes), BF16),
+            vmem((rows, count, lanes), BF16),
             vmem((rows, count, lanes), BF16),
             vmem((rows, count, lanes), BF16),
             vmem((3 * rows, count + 2 * EDGE, lanes), F32),

time: 60.4 us -> 55.8 us (0.924)
  the two profiles are of different devices: /device:TPU:56 before, /device:TPU:2 now
where the time goes in v3:
time: 55.8 us; the launch traced here: 55.7 us
  Pallas kernels  55.1 us (99%)
  between operations  0.64 us (1%)
    pallas_call x1, Pallas kernels, per_device(): pl.pallas_call(functools.partial(kernel, count), out_shape=tuple((pltpu.V...  54.2 us

profile of v3, /device:TPU:2, one launch (start us, length us, event | category | flops | bytes accessed | tf_op | source)
XLA Modules:
  0.0 55.7 jit_solution(11046654195348878275)
XLA Ops:
  0.6 54.2 %global_filter.1 = (bf16[3,128,128]{2,1,0:T(8,128)(2,1)S(1)}, bf16[3,128,128]{2,1,0:T(8,128)(2,1)S(1)}, f32[2,384,128]{2,1,0:T(8,128)S(1)}, f32[7,7,128]{2,1,0:T(8,128)S(1)}) custom-call(bf16[3,128,128]{2,1,0:T(8,128)(2,1)} %tok_hbm.1, f32[7,7,128]{2,1,0:T(8,128)} %weight_hbm.1, bf16[2,384,128]{2,1,0:T(8,128)(2,1)} %bitcast.4, bf16[3,128,128]{2,1,0:T(8,128)(2,1)} %cot_hbm.1, ...), custom_call_target="tpu_custom_call" | custom-call | tf_op jit(solution)/shard_map/global_filter/pallas_call | solution.py:370
  54.9 0.9 %deliver.1 = (bf16[3,128,128]{2,1,0:T(8,128)(2,1)}, bf16[3,128,128]{2,1,0:T(8,128)(2,1)}, f32[2,384,128]{2,1,0:T(8,128)}, f32[7,7,128]{2,1,0:T(8,128)}) custom-call(bf16[3,128,128]{2,1,0:T(8,128)(2,1)S(1)} %get-tuple-element.12.refs_0_, bf16[3,128,128]{2,1,0:T(8,128)(2,1)S(1)} %get-tuple-element.13.refs_1_, f32[2,384,128]{2,1,0:T(8,128)S(1)} %get-tuple-element.14.refs_2_, ...), custom_call_target="tpu_custom_call" | custom-call | tf_op jit(solution)/shard_map/deliver/pallas_call | solution.py:404

commit v4 on v3

--- a/solution.py
+++ b/solution.py
@@ -19,7 +19,7 @@
 EDGE = 8
 CHUNK = 32
 QUARTERS = 4
-ORDER = (2, 1, 3, 0)
+ORDER = (2, 3, 1, 0)
 
 
 def halves(table):
@@ -85,7 +85,7 @@
     home = me // quarter
 
     def peers(shift):
-        base = jnp.bitwise_and(home + shift, QUARTERS - 1) * quarter
+        base = jnp.bitwise_xor(home, shift) * quarter
         for i in range(1 if shift == 0 else 0, quarter):
             yield base + jnp.bitwise_and(me + i, quarter - 1)
 
@@ -93,26 +93,29 @@
         for target in peers(shift):
             pl.semaphore_signal(barrier, 1, device_id={"row": target})
 
-    def scatter(slot, table_parts, wait=None):
-        for shift in ORDER:
-            base = jnp.bitwise_and(home + shift, QUARTERS - 1)
-            rows = pl.ds(pl.multiple_of(base * (quarter * SLOT), quarter * SLOT), quarter * SLOT)
+    def scatter(slot, table_parts, groups=1, wait=None):
+        span = QUARTERS // groups
+        for group in range(groups):
+            shifts = ORDER[group * span : (group + 1) * span]
+            base = jnp.bitwise_and(jnp.bitwise_xor(home, shifts[0]), QUARTERS - span) if groups > 1 else 0
+            size = span * quarter * SLOT
+            rows = pl.ds(pl.multiple_of(base * (quarter * SLOT), size), size)
             total = None
             for table, value in table_parts:
                 term = dot(table[rows, :], value)
                 total = term if total is None else total + term
-            send[slot, pl.ds(base * quarter, quarter)] = total.reshape(quarter, SLOT, 128).astype(BF16)
+            send[slot, pl.ds(base * quarter, span * quarter)] = total.reshape(span * quarter, SLOT, 128).astype(BF16)
             if wait is not None:
                 wait()
-                wait = None
-            for target in peers(shift):
-                pltpu.make_async_remote_copy(
-                    send.at[slot, target, pl.ds(0, USED)],
-                    recv.at[slot, me, pl.ds(0, USED)],
-                    send_sem.at[slot],
-                    recv_sem.at[slot],
-                    device_id={"row": target},
-                ).start()
+            for shift in shifts:
+                for target in peers(shift):
+                    pltpu.make_async_remote_copy(
+                        send.at[slot, target, pl.ds(0, USED)],
+                        recv.at[slot, me, pl.ds(0, USED)],
+                        send_sem.at[slot],
+                        recv_sem.at[slot],
+                        device_id={"row": target},
+                    ).start()
         recv[slot, pl.ds(me, 1)] = send[slot, pl.ds(me, 1)]
 
     def all_of(slot):
@@ -197,7 +200,7 @@
     for load in loads[:3]:
         load.wait()
     value = cot[...].reshape(ROWS * count, 128)
-    scatter(0, ((c1h, value), (c1l, value)), enter)
+    scatter(0, ((c1h, value), (c1l, value)), wait=enter)
 
     @pl.when(me > 0)
     def _():
@@ -228,7 +231,7 @@
     back = jnp.concatenate(
         [(cot_re * filt_re + cot_im * filt_im).astype(BF16), (cot_im * filt_re - cot_re * filt_im).astype(BF16)]
     )
-    scatter(2, ((r3, back),))
+    scatter(2, ((r3, back),), groups=2)
 
     loads[8].wait()
     loads[9].wait()

time: 55.8 us -> 54.6 us (0.978)
  the two profiles are of different devices: /device:TPU:2 before, /device:TPU:56 now
where the time goes in v4:
time: 54.6 us; the launch traced here: 54.3 us
  Pallas kernels  53.7 us (98%)
  between operations  0.64 us (1%)
    pallas_call x1, Pallas kernels, per_device(): pl.pallas_call(functools.partial(kernel, count), out_shape=tuple((pltpu.V...  52.8 us

profile of v4, /device:TPU:56, one launch (start us, length us, event | category | flops | bytes accessed | tf_op | source)
XLA Modules:
  0.0 54.3 jit_solution(253123261780204065)
XLA Ops:
  0.6 52.8 %global_filter.1 = (bf16[3,128,128]{2,1,0:T(8,128)(2,1)S(1)}, bf16[3,128,128]{2,1,0:T(8,128)(2,1)S(1)}, f32[2,384,128]{2,1,0:T(8,128)S(1)}, f32[7,7,128]{2,1,0:T(8,128)S(1)}) custom-call(bf16[3,128,128]{2,1,0:T(8,128)(2,1)} %tok_hbm.1, f32[7,7,128]{2,1,0:T(8,128)} %weight_hbm.1, bf16[2,384,128]{2,1,0:T(8,128)(2,1)} %bitcast.4, bf16[3,128,128]{2,1,0:T(8,128)(2,1)} %cot_hbm.1, ...), custom_call_target="tpu_custom_call" | custom-call | tf_op jit(solution)/shard_map/global_filter/pallas_call | solution.py:373
  53.5 0.9 %deliver.1 = (bf16[3,128,128]{2,1,0:T(8,128)(2,1)}, bf16[3,128,128]{2,1,0:T(8,128)(2,1)}, f32[2,384,128]{2,1,0:T(8,128)}, f32[7,7,128]{2,1,0:T(8,128)}) custom-call(bf16[3,128,128]{2,1,0:T(8,128)(2,1)S(1)} %get-tuple-element.12.refs_0_, bf16[3,128,128]{2,1,0:T(8,128)(2,1)S(1)} %get-tuple-element.13.refs_1_, f32[2,384,128]{2,1,0:T(8,128)S(1)} %get-tuple-element.14.refs_2_, ...), custom_call_target="tpu_custom_call" | custom-call | tf_op jit(solution)/shard_map/deliver/pallas_call | solution.py:407

commit v5 on v4

--- a/solution.py
+++ b/solution.py
@@ -264,6 +264,7 @@
         pltpu.make_async_remote_copy(
             part.at[peer], by_depth.at[i], sum_send.at[0], sum_recv.at[0], device_id={"row": peer * plane + plane_at}
         ).start()
+    start_rims(field_up, field_down)
 
     sums(part.at[others], by_depth.at[others], 0).wait_recv()
     total = part[depth_at]
@@ -277,8 +278,6 @@
             by_plane.at[plane_at], by_plane.at[plane_at], sum_send.at[1], sum_recv.at[1],
             device_id={"row": depth_at * plane + peer},
         ).start()
-
-    start_rims(field_up, field_down)
 
     spec[...] = dot(r2[...], gathered(1))
     spec_re, spec_im = spec[0:height, :], spec[height : 2 * height, :]

time: 54.6 us -> 54.8 us (level)
  no operation moved by 1% of the time
where the time goes in v5:
time: 54.8 us; the launch traced here: 54.7 us
  Pallas kernels  54.1 us (99%)
  between operations  0.64 us (1%)
    pallas_call x1, Pallas kernels, per_device(): pl.pallas_call(functools.partial(kernel, count), out_shape=tuple((pltpu.V...  53.2 us

profile of v5, /device:TPU:56, one launch (start us, length us, event | category | flops | bytes accessed | tf_op | source)
XLA Modules:
  0.0 54.7 jit_solution(11840448925047580573)
XLA Ops:
  0.6 53.2 %global_filter.1 = (bf16[3,128,128]{2,1,0:T(8,128)(2,1)S(1)}, bf16[3,128,128]{2,1,0:T(8,128)(2,1)S(1)}, f32[2,384,128]{2,1,0:T(8,128)S(1)}, f32[7,7,128]{2,1,0:T(8,128)S(1)}) custom-call(bf16[3,128,128]{2,1,0:T(8,128)(2,1)} %tok_hbm.1, f32[7,7,128]{2,1,0:T(8,128)} %weight_hbm.1, bf16[2,384,128]{2,1,0:T(8,128)(2,1)} %bitcast.4, bf16[3,128,128]{2,1,0:T(8,128)(2,1)} %cot_hbm.1, ...), custom_call_target="tpu_custom_call" | custom-call | tf_op jit(solution)/shard_map/global_filter/pallas_call | solution.py:372
  53.9 0.9 %deliver.1 = (bf16[3,128,128]{2,1,0:T(8,128)(2,1)}, bf16[3,128,128]{2,1,0:T(8,128)(2,1)}, f32[2,384,128]{2,1,0:T(8,128)}, f32[7,7,128]{2,1,0:T(8,128)}) custom-call(bf16[3,128,128]{2,1,0:T(8,128)(2,1)S(1)} %get-tuple-element.12.refs_0_, bf16[3,128,128]{2,1,0:T(8,128)(2,1)S(1)} %get-tuple-element.13.refs_1_, f32[2,384,128]{2,1,0:T(8,128)S(1)} %get-tuple-element.14.refs_2_, ...), custom_call_target="tpu_custom_call" | custom-call | tf_op jit(solution)/shard_map/deliver/pallas_call | solution.py:406
